TPU v7x, 512 devices: a whole 4x4x16 slice. The times are simulated.
512 devices in a mesh: ctx: 64 (over z, x), ch: 8 (over y, core).
Axes of the slice: x: 4, y: 4, z: 16, core: 2. Of those that a mesh axis runs over, the one named last changes fastest.
Arguments:
- gate_input: bfloat16 [16384, 4096], P('ctx', 'ch'), may hold values from -6 to 6
- key_input: bfloat16 [16384, 4096], P('ctx', 'ch'), may hold values from -6 to 6
- value_input: bfloat16 [16384, 4096], P('ctx', 'ch'), may hold values from -6 to 6
- decay_rate: float32 [16, 4096], P(None, 'ch'), may hold values from 0.00012207031 to 0.26666667
- frequency: float32 [16, 4096], P(None, 'ch'), may hold values from 0 to 2.4
- residue: float32 [2, 16, 4096], P(None, None, 'ch'), may hold values from -2 to 2
- skip_gain: float32 [4096], P('ch'), may hold values from -3 to 3
- out_weight: bfloat16 [4096, 4096], P('ctx', 'ch'), may hold values from -0.09375 to 0.09375
Outputs:
- mixed: bfloat16 [16384, 4096], P('ctx', 'ch')
All inputs are finite; a program needn't handle non-finite values.
Results may differ from a plain program's by a relative error of at most 0.014.
Values may be sent and summed in bfloat16 or wider, within the bound.
A program may use at most 128 MiB of HBM per device.

v0:
```python
import jax
import jax.numpy as jnp
from jax import lax
from jax.sharding import PartitionSpec as P


def entering(value, axis, join, neutral):
    count, mine = (lax.axis_size(axis), lax.axis_index(axis))
    pieces = jax.tree.map(lambda part: lax.all_gather(part, axis), value)
    so_far = jax.tree.map(
        lambda part, zero: jnp.full_like(part, 0) + jnp.asarray(zero, part.dtype), value, neutral
    )

    def hop(position, so_far):
        longer = join(so_far, jax.tree.map(lambda part: part[position], pieces))
        return jax.tree.map(lambda new, old: jnp.where(position < mine, new, old), longer, so_far)

    return lax.fori_loop(0, count - 1, hop, so_far)


def cmul(a_re, a_im, b_re, b_im):
    return (a_re * b_re - a_im * b_im, a_re * b_im + a_im * b_re)


def filter_tables(decay_rate, frequency, residue, block_len):
    damping = 0.125 * decay_rate
    turning = 0.125 * frequency
    scaling = jnp.sqrt(2.0 * damping)
    coef_re = scaling * residue[0]
    coef_im = scaling * residue[1]
    offsets = jnp.arange(block_len).astype(jnp.float32)

    def powers(counts):
        fading = jnp.exp(-damping[None] * counts[:, None, None])
        phase = turning[None] * counts[:, None, None]
        return (fading * jnp.cos(phase), fading * jnp.sin(phase))

    back_re, back_im = powers(block_len - 1.0 - offsets)
    ahead_re, ahead_im = powers(offsets + 1.0)
    out_re, out_im = cmul(coef_re[None], coef_im[None], ahead_re, ahead_im)
    lag_re, lag_im = powers(offsets)
    filt = jnp.sum(coef_re[None] * lag_re - coef_im[None] * lag_im, axis=1)
    places = jnp.arange(block_len)
    differ = places[:, None] - places[None, :]
    picked = jnp.take(filt, jnp.maximum(differ, 0), axis=0)
    toeplitz = jnp.where((differ >= 0)[:, :, None], picked, jnp.zeros_like(picked))
    jump_re, jump_im = powers(jnp.full((1,), block_len).astype(jnp.float32))
    return (back_re, back_im, out_re, out_im, toeplitz, jump_re[0], jump_im[0])


def chain(earlier, later):
    sum_re, sum_im = cmul(earlier[0], earlier[1], later[2], later[3])
    pow_re, pow_im = cmul(earlier[2], earlier[3], later[2], later[3])
    return (sum_re + later[0], sum_im + later[1], pow_re, pow_im)


def on_device(
    gate_input, key_input, value_input, decay_rate, frequency, residue, skip_gain, out_weight
):
    highest = lax.Precision.HIGHEST
    signal = key_input.astype(jnp.float32) * value_input.astype(jnp.float32)
    tok_len, chans = signal.shape
    block_len = 16
    block_count = tok_len // block_len
    back_re, back_im, out_re, out_im, toeplitz, jump_re, jump_im = filter_tables(
        decay_rate, frequency, residue, block_len
    )
    blocks = signal.reshape(block_count, block_len, chans)
    entry_re = jnp.einsum("snc,bsc->bnc", back_re, blocks, precision=highest)
    entry_im = jnp.einsum("snc,bsc->bnc", back_im, blocks, precision=highest)

    def advance(state, entry):
        moved_re, moved_im = cmul(jump_re, jump_im, state[0], state[1])
        grown_re, grown_im = cmul(state[2], state[3], jump_re, jump_im)
        return ((moved_re + entry[0], moved_im + entry[1], grown_re, grown_im), state)

    zeros = jnp.zeros(jump_re.shape, jnp.float32)
    ones = jnp.ones(jump_re.shape, jnp.float32)
    final, starts = lax.scan(advance, (zeros, zeros, ones, zeros), (entry_re, entry_im))
    local_re, local_im, device_re, device_im = final
    prefix = entering(
        (local_re, local_im, device_re, device_im), "ctx", chain, (zeros, zeros, ones, zeros)
    )
    incoming_re, incoming_im = (prefix[0], prefix[1])
    carried_re, carried_im = cmul(starts[2], starts[3], incoming_re[None], incoming_im[None])
    begin_re = starts[0] + carried_re
    begin_im = starts[1] + carried_im
    far = jnp.einsum("tnc,bnc->btc", out_re, begin_re, precision=highest) - jnp.einsum(
        "tnc,bnc->btc", out_im, begin_im, precision=highest
    )
    near = jnp.einsum("tsc,bsc->btc", toeplitz, blocks, precision=highest)
    conv = (near + far).reshape(tok_len, chans)
    gated = (gate_input.astype(jnp.float32) * (conv + skip_gain[None, :] * signal)).astype(
        jnp.bfloat16
    )
    whole = lax.all_gather(gated, "ch", axis=1, tiled=True)
    all_rows = lax.all_gather(out_weight, "ctx", axis=0, tiled=True)
    mixed = jnp.dot(whole, all_rows, preferred_element_type=jnp.float32)
    return mixed.astype(jnp.bfloat16)


def solution(mesh):
    placed = (
        P("ctx", "ch"),
        P("ctx", "ch"),
        P("ctx", "ch"),
        P(None, "ch"),
        P(None, "ch"),
        P(None, None, "ch"),
        P("ch"),
        P("ctx", "ch"),
    )
    return jax.shard_map(
        on_device, mesh=mesh, in_specs=placed, out_specs=P("ctx", "ch"), check_vma=False
    )
```

profile of v0, /device:TPU:16, one launch (start us, length us, event | category | flops | bytes accessed | tf_op | source)
XLA Modules:
  0.0 906.4 jit_solution(10265172625318404622)
XLA Ops:
  6.6 1.1 convert_multiply_fusion
  7.7 3.7 copy.51
  11.5 6.1 multiply_add_fusion.1
  17.6 4.1 copy.54
  21.8 9.9 %convolution_bitcast_fusion.1 = f32[16,16,512]{1,0,2:T(8,128)} fusion(f32[16,16,512]{1,0,2:T(8,128)} %copy.51, f32[16,16,512]{1,0,2:T(8,128)} %copy.54), kind=kOutput, calls=%fused_computation.21 | convolution fusion | flops 25165824 | bytes 1572864 | tf_op jit(solution)/shard_map/snc,bsc->bnc/dot_general | solution.py:69
  31.7 3.5 copy.57
  35.2 3.7 copy.56
  38.9 9.9 %convolution_bitcast_fusion = f32[16,16,512]{1,0,2:T(8,128)} fusion(f32[16,16,512]{1,0,2:T(8,128)} %copy.51, f32[16,16,512]{1,0,2:T(8,128)} %copy.56), kind=kOutput, calls=%fused_computation.20 | convolution fusion | flops 25165824 | bytes 1572864 | tf_op jit(solution)/shard_map/snc,bsc->bnc/dot_general | solution.py:70
  48.8 3.5 copy.58
  52.5 14.0 %while.41 = (s32[]{:T(128)}, f32[16,512]{1,0:T(8,128)S(1)}, f32[16,512]{1,0:T(8,128)S(1)}, f32[16,512]{1,0:T(8,128)S(1)}, f32[16,512]{1,0:T(8,128)S(1)}, /*index...) while((s32[]{:T(128)}, f32[16,512]{1,0:T(8,128)S(1)}, ...), condition=%wide.region_2.3_spmd.clone, body=%wide.region_1.2_spmd.clone.sunk | while | flops 180227 | bytes 655533 | solution.py:79
  69.6 1.8 gather_fusion
  71.4 2.0 select_select_fusion
  73.4 4.5 copy.52
  77.9 3.6 copy.60
  81.5 3.7 copy.62
  85.2 12.3 %fusion.17 = f32[512,16,16]{2,1,0:T(8,128)} fusion(f32[16,16,512]{1,0,2:T(8,128)} %copy.51, f32[16,16,512]{1,0,2:T(8,128)} %copy.52), kind=kOutput, calls=%fused_computation.66 | convolution fusion | flops 25165824 | bytes 1572864 | tf_op jit(solution)/shard_map/tsc,bsc->btc/dot_general | solution.py:91
  97.5 115.1 %all-gather.15.cloned.1.call-done = f32[1024,512]{1,0:T(8,128)} async-done(((f32[16,512]{1,0:T(8,128)}), f32[1024,512]{1,0:T(8,128)}) %all-gather.15.cloned.1.call-update) | async-done | bytes 2097168 | tf_op jit(solution)/shard_map/all_gather | solution.py:9
  212.6 139.9 %all-gather.17.cloned.1.call-done = f32[1024,512]{1,0:T(8,128)} async-done(((f32[16,512]{1,0:T(8,128)}), f32[1024,512]{1,0:T(8,128)}) %all-gather.17.cloned.1.call-update) | async-done | bytes 2097168 | tf_op jit(solution)/shard_map/all_gather | solution.py:9
  352.5 139.9 %all-gather.19.cloned.1.call-done = f32[1024,512]{1,0:T(8,128)} async-done(((f32[16,512]{1,0:T(8,128)}), f32[1024,512]{1,0:T(8,128)}) %all-gather.19.cloned.1.call-update) | async-done | bytes 2097168 | tf_op jit(solution)/shard_map/all_gather | solution.py:9
  492.4 139.8 %all-gather.21.cloned.1.call-done = f32[1024,512]{1,0:T(8,128)} async-done(((f32[16,512]{1,0:T(8,128)}), f32[1024,512]{1,0:T(8,128)}) %all-gather.21.cloned.1.call-update) | async-done | bytes 2097168 | tf_op jit(solution)/shard_map/all_gather | solution.py:9
  632.2 54.2 %while.42 = (s32[]{:T(128)}, f32[16,512]{1,0:T(8,128)S(1)}, f32[16,512]{1,0:T(8,128)S(1)}, s32[]{:T(128)}, f32[64,16,512]{2,1,0:T(8,128)}, /*index=5*/f32[64,16,...) while((s32[]{:T(128)}, f32[16,512]{1,0:T(8,128)S(1)}, ...), condition=%wide.region_4.5_spmd.clone, body=%wide.region_3.4_spmd.clone.sunk | while | flops 98308 | bytes 262277 | solution.py:18
  643.4 0.9 fusion.32
  644.3 0.8 fusion.32
  645.1 0.8 fusion.32
  646.0 0.8 fusion.32
  646.8 0.8 fusion.32
  647.7 0.8 fusion.32
  648.6 0.8 fusion.32
  649.4 0.8 fusion.32
  650.3 0.8 fusion.32
  651.1 0.8 fusion.32
  652.0 0.8 fusion.32
  652.9 0.8 fusion.32
  653.7 0.8 fusion.32
  654.6 0.8 fusion.32
  655.4 0.8 fusion.32
  656.3 0.8 fusion.32
  657.2 0.8 fusion.32
  658.0 0.8 fusion.32
  658.9 0.8 fusion.32
  659.7 0.8 fusion.32
  660.6 0.8 fusion.32
  661.5 0.8 fusion.32
  662.3 0.8 fusion.32
  663.2 0.8 fusion.32
  664.0 0.8 fusion.32
  664.9 0.8 fusion.32
  665.8 0.8 fusion.32
  666.6 0.8 fusion.32
  667.5 0.8 fusion.32
  668.3 0.8 fusion.32
  669.2 0.8 fusion.32
  670.1 0.8 fusion.32
  670.9 0.8 fusion.32
  671.8 0.8 fusion.32
  686.7 3.7 copy.59
  690.4 3.6 copy.61
  694.0 9.5 %fusion.18 = f32[512,16,16]{2,1,0:T(8,128)S(1)} fusion(f32[16,16,512]{1,0,2:T(8,128)} %copy.59, f32[16,16,512]{1,0,2:T(8,128)} %copy.60), kind=kOutput, calls=%fused_computation.67 | convolution fusion | flops 25165824 | bytes 1572864 | tf_op jit(solution)/shard_map/tnc,bnc->btc/dot_general | solution.py:88
  703.5 8.5 add_bitcast_fusion
  712.0 2.9 copy.63
  714.9 0.8 fusion.15
  716.4 27.4 %all-gather.11.cloned.1.call-done = bf16[256,4096]{1,0:T(8,128)(2,1)} async-done(((bf16[256,512]{1,0:T(8,128)(2,1)}), bf16[256,4096]{1,0:T(8,128)(2,1)}) %all-gather.11.cloned.1.call-update) | async-done | bytes 2097168 | tf_op jit(solution)/shard_map/all_gather | solution.py:96
  743.8 150.7 %all-gather.13.cloned.1.call-done = bf16[4096,512]{1,0:T(8,128)(2,1)} async-done(((bf16[64,512]{1,0:T(8,128)(2,1)}), bf16[4096,512]{1,0:T(8,128)(2,1)}) %all-gather.13.cloned.1.call-update) | async-done | bytes 4194320 | tf_op jit(solution)/shard_map/all_gather | solution.py:97
  894.6 4.8 convolution_convert_fusion
  (135 shorter events, 41.9 us)
Async XLA Ops:
  6.5 4.8 copy-start.11
  6.5 4.8 copy-start.12
  6.5 4.8 copy-start.10
  6.5 206.0 %all-gather.15.cloned.1.call-start = ((), (), s32[]{:S(2)}) async-start(), calls=%async_computation.2 | async-start | bytes 2129920 | tf_op jit(solution)/shard_map/all_gather | solution.py:9
  66.5 0.6 copy-start.5
  66.6 0.7 copy-start.6
  66.6 1.4 copy-start.3
  66.6 2.1 copy-start.4
  67.2 285.3 %all-gather.17.cloned.1.call-start = ((), (), s32[]{:S(2)}) async-start(), calls=%async_computation.3 | async-start | bytes 2129920 | tf_op jit(solution)/shard_map/all_gather | solution.py:9
  67.9 424.5 %all-gather.19.cloned.1.call-start = ((), (), s32[]{:S(2)}) async-start(), calls=%async_computation.4 | async-start | bytes 2129920 | tf_op jit(solution)/shard_map/all_gather | solution.py:9
  68.7 563.5 %all-gather.21.cloned.1.call-start = ((), (), s32[]{:S(2)}) async-start(), calls=%async_computation.5 | async-start | bytes 2129920 | tf_op jit(solution)/shard_map/all_gather | solution.py:9
  69.2 674.6 %all-gather.11.cloned.1.call-start = ((), (), s32[]{:S(2)}) async-start(), calls=%async_computation | async-start | bytes 2359296 | tf_op jit(solution)/shard_map/all_gather | solution.py:96
  694.0 9.5 %copy-start = (f32[512,16,16]{2,1,0:T(8,128)S(1)}, f32[512,16,16]{2,1,0:T(8,128)}, u32[]{:S(2)}) copy-start(f32[512,16,16]{2,1,0:T(8,128)} %fusion.17) | copy-start | bytes 1572868
  694.0 9.5 %copy-start.1 = (f32[16,16,512]{1,0,2:T(8,128)S(1)}, f32[16,16,512]{1,0,2:T(8,128)}, u32[]{:S(2)}) copy-start(f32[16,16,512]{1,0,2:T(8,128)} %copy.62) | copy-start | bytes 1572868
  694.0 9.5 %copy-start.2 = (f32[16,16,512]{1,0,2:T(8,128)S(1)}, f32[16,16,512]{1,0,2:T(8,128)}, u32[]{:S(2)}) copy-start(f32[16,16,512]{1,0,2:T(8,128)} %copy.61) | copy-start | bytes 1572868
  712.0 2.9 copy-start.7
  712.0 2.9 copy-start.8
  712.0 2.9 copy-start.9
  712.0 2.9 copy-start.13
  715.8 178.7 %all-gather.13.cloned.1.call-start = ((), (), s32[]{:S(2)}) async-start(), calls=%async_computation.1 | async-start | bytes 4259840 | tf_op jit(solution)/shard_map/all_gather | solution.py:97
Sparse Core Ops, SparseCore 0:
  67.3 145.2 all-gather.14
  215.5 136.9 all-gather.16
  355.4 136.9 all-gather.18
  495.2 136.9 all-gather.20
  715.9 27.8 all-gather.10
  746.6 147.8 all-gather.12
where the time goes:
time: 918 us; the launch traced here: 906 us
  waiting for transfers between devices  715 us (78%)
  other arithmetic  76.7 us (8%)
  matrix products  54.8 us (6%)
  local copies, waits for them, and re-layouts  43.3 us (5%)
  between operations  14 us (2%)
    all_gather x4, waiting for transfers between devices, entering(): pieces = jax.tree.map(lambda part: lax.all_gather(part, axis), value)  535 us
    all_gather x1, waiting for transfers between devices, on_device(): all_rows = lax.all_gather(out_weight, 'ctx', axis=0, tiled=True)  151 us
    select_n x63, other arithmetic, hop(): jnp.where(position < mine, new, old)  52.8 us
    all_gather x1, waiting for transfers between devices, on_device(): whole = lax.all_gather(gated, 'ch', axis=1, tiled=True)  27.4 us
    add x17, other arithmetic, cmul(): return (a_re * b_re - a_im * b_im, a_re * b_im + a_im * b_re)  19.1 us
  transfers between devices with their start and end apart: 6, of which 6 were waited for; matrix products, arithmetic and copies ran while one was open for 3% of the time, Pallas kernels for 0%

commit v1 on v0

v1 whole, which is shorter than its diff:
```python
import functools

import jax
import jax.numpy as jnp
from jax import lax
from jax.experimental import pallas as pl
from jax.experimental.pallas import tpu as pltpu
from jax.sharding import PartitionSpec as P

MESH = pl.DeviceIdType.MESH
NX = 4
L = 16


def cmul(a_re, a_im, b_re, b_im):
    return (a_re * b_re - a_im * b_im, a_re * b_im + a_im * b_re)


def remote(src, dst, send_sem, recv_sem, device):
    return pltpu.make_async_remote_copy(
        src_ref=src,
        dst_ref=dst,
        send_sem=send_sem,
        recv_sem=recv_sem,
        device_id=device,
        device_id_type=MESH,
    )


def kernel(
    cfg,
    gate, key, value, decay, freq, residue, skip, weight,
    out,
    wfull, gall, sig, near, acc,
    pow_re, pow_im, out_re, out_im, toep, hpad,
    ent_re, ent_im, beg_re, beg_im, co_re, co_im,
    esend, esum, qpow, xin, zin, zin2, rsum, wsum, sx, sin,
    ax_s, ax_r, az_s, az_r, bz_s, bz_r, bx_s, bx_r, bh_s, bh_r,
    st_s, st_r, y_s, y_r,
):
    nz, ny, radix = cfg
    tok, chans = key.shape
    blocks = tok // L
    lanes = chans // NX
    rows = weight.shape[0]
    ra = rows // 2
    half = ra + (rows - ra) // 2
    zlim = ((1, nz // 2), (-1, nz // 2 - 1))

    ctx = lax.axis_index("ctx")
    ch = lax.axis_index("ch")
    z, x = ctx // NX, lax.rem(ctx, NX)
    y, core = ch // 2, lax.rem(ch, 2)

    def at_z(d):
        return (lax.rem(z + d + nz, nz) * NX + x, ch)

    def at_x(d):
        return (z * NX + lax.rem(x + d + NX, NX), ch)

    def at_y(d):
        return (ctx, lax.rem(y + d + ny, ny) * 2 + core)

    other = (ctx, y * 2 + 1 - core)

    near_z = list(range(1, radix))
    far_z = [1 + radix * m for m in range(radix)]
    z_peers = sorted({d % nz for d in [1, nz - 1] + near_z + far_z + [-d for d in near_z + far_z]})
    peers = [at_z(d) for d in z_peers] + [at_x(d) for d in range(1, NX)]
    if ny > 1:
        peers += [at_y(1), at_y(-1), other]
    barrier = pltpu.get_barrier_semaphore()
    for peer in peers:
        pl.semaphore_signal(barrier, inc=1, device_id=peer, device_id_type=MESH)

    wfull[ctx] = weight[...]
    damp = 0.125 * decay[...]
    turn = 0.125 * freq[...]
    fade = jnp.exp(-damp)
    lam_re, lam_im = fade * jnp.cos(turn), fade * jnp.sin(turn)
    scale = jnp.sqrt(2.0 * damp)
    co_re[...] = scale * residue[0]
    co_im[...] = scale * residue[1]
    cur = (jnp.ones_like(lam_re), jnp.zeros_like(lam_im))
    for k in range(L + 1):
        pow_re[k] = cur[0]
        pow_im[k] = cur[1]
        cur = cmul(cur[0], cur[1], lam_re, lam_im)

    pl.semaphore_wait(barrier, len(peers))

    def a_first(d):
        part = wfull.at[ctx, 0:ra]
        return remote(part, part, ax_s.at[d - 1], ax_r.at[d - 1], at_x(d))

    def a_step(dirn, k, sub, sgn, src_z):
        part = wfull.at[pl.ds(src_z * NX + 2 * sub, 2), 0:ra]
        return remote(part, part, az_s.at[dirn, k, sub], az_r.at[dirn, k, sub], at_z(sgn))

    def bz_step(dirn, k, sgn, src_z):
        part = wfull.at[src_z * NX + x, ra:rows]
        return remote(part, part, bz_s.at[dirn, k], bz_r.at[dirn, k], at_z(sgn))

    def bx_step(idx, src_z, side, from_x):
        part = wfull.at[src_z * NX + lax.rem(from_x + NX, NX), ra:rows]
        return remote(part, part, bx_s.at[idx, side], bx_r.at[idx, side], at_x(1 - 2 * side))

    def bh_step(idx, src_z, side, from_x):
        span = slice(ra, half) if side == 0 else slice(half, rows)
        part = wfull.at[src_z * NX + lax.rem(from_x + NX, NX), span]
        return remote(part, part, bh_s.at[idx, side], bh_r.at[idx, side], at_x(1 - 2 * side))

    def origin(sgn, k):
        return lax.rem(z - sgn * k + nz, nz)

    def halves(idx, src_z):
        for side in range(2):
            here = x - 1 if side == 0 else x + 1
            bx_step(idx, src_z, side, here).wait_recv()
            bh_step(idx, src_z, side, here).start()

    for d in (1, 3, 2):
        a_first(d).start()
    for dirn, (sgn, lim) in enumerate(zlim):
        bz_step(dirn, 1, sgn, z).start()
    for side in range(2):
        bx_step(0, z, side, x).start()

    jump_re, jump_im = pow_re[L], pow_im[L]
    esum[0] = jnp.zeros_like(jump_re)
    esum[1] = jnp.zeros_like(jump_re)

    def entries(b, _):
        at = pl.multiple_of(b * L, L)
        sig[pl.ds(at, L), :] = key[pl.ds(at, L), :].astype(jnp.float32) * value[
            pl.ds(at, L), :
        ].astype(jnp.float32)
        e_re = jnp.zeros(jump_re.shape, jnp.float32)
        e_im = jnp.zeros(jump_re.shape, jnp.float32)
        for s in range(L):
            row = sig[pl.ds(at + s, 1), :]
            e_re += pow_re[L - 1 - s] * row
            e_im += pow_im[L - 1 - s] * row
        ent_re[b] = e_re
        ent_im[b] = e_im
        m_re, m_im = cmul(pow_re[L], pow_im[L], esum[0], esum[1])
        esum[0] = m_re + e_re
        esum[1] = m_im + e_im
        return 0

    lax.fori_loop(0, blocks, entries, 0)
    for q in range(NX):
        for part in range(2):
            esend[q, part] = esum[part, :, q * lanes : (q + 1) * lanes]

    def x_out(d):
        to = lax.rem(x + d, NX)
        return remote(esend.at[to], xin.at[x], st_s.at[d - 1], st_r.at[d - 1], at_x(d))

    def z_out(i):
        d = near_z[i]
        return remote(rsum, zin.at[i], st_s.at[3 + i], st_r.at[3 + i], at_z(d))

    def z_out2(i):
        return remote(wsum, zin2.at[i], st_s.at[6 + i], st_r.at[6 + i], at_z(far_z[i]))

    def x_back(d):
        to = lax.rem(x + d, NX)
        return remote(sx.at[to], sin.at[x], st_s.at[9 + d], st_r.at[9 + d], at_x(d))

    for d in (1, 3, 2):
        x_out(d).start()
    xin[x] = esend[x]

    for d in (1, 3, 2):
        a_first(d).wait_recv()
    for dirn, (sgn, lim) in enumerate(zlim):
        for sub in range(2):
            a_step(dirn, 1, sub, sgn, z).start()

    fade_q = jnp.exp(-damp * float(tok))
    q_re = fade_q * jnp.cos(turn * float(tok))
    q_im = fade_q * jnp.sin(turn * float(tok))
    for q in range(NX):
        qpow[q, 0] = q_re[:, q * lanes : (q + 1) * lanes]
        qpow[q, 1] = q_im[:, q * lanes : (q + 1) * lanes]

    place = lax.broadcasted_iota(jnp.int32, (8, chans), 0)

    def out_tables(n, total):
        def row(ref, k):
            return jnp.broadcast_to(ref[k, pl.ds(n, 1), :], (8, chans))

        c_re = jnp.broadcast_to(co_re[pl.ds(n, 1), :], (8, chans))
        c_im = jnp.broadcast_to(co_im[pl.ds(n, 1), :], (8, chans))
        v = cmul(c_re, c_im, row(pow_re, 1), row(pow_im, 1))
        for bit in (1, 2, 4):
            w = cmul(*v, row(pow_re, bit), row(pow_im, bit))
            on = (place & bit) != 0
            v = (jnp.where(on, w[0], v[0]), jnp.where(on, w[1], v[1]))
        hi = cmul(*v, row(pow_re, 8), row(pow_im, 8))
        t_re = jnp.concatenate([v[0], hi[0]], axis=0)
        out_re[n] = t_re
        out_im[n] = jnp.concatenate([v[1], hi[1]], axis=0)
        return total + t_re

    def filters():
        later = lax.fori_loop(
            0, 16, out_tables, jnp.zeros((L, chans), jnp.float32)
        )
        hpad[0:L, :] = jnp.zeros((L, chans), jnp.float32)
        hpad[L - 1 : L, :] = jnp.sum(co_re[...], axis=0, keepdims=True) + skip[...]
        hpad[L : 2 * L, :] = later
        for s in range(L):
            toep[s] = hpad[L - 1 - s : 2 * L - 1 - s, :]

    def near_part(b, _):
        at = pl.multiple_of(b * L, L)
        total = jnp.zeros((L, chans), jnp.float32)
        for s in range(L):
            total += toep[s] * sig[pl.ds(at + s, 1), :]
        near[pl.ds(at, L), :] = total
        return 0

    def quarter_power(exp):
        one = (qpow[x, 0], qpow[x, 1])
        got = None
        while exp:
            if exp & 1:
                got = one if got is None else cmul(*got, *one)
            one = cmul(*one, *one)
            exp >>= 1
        return got

    def stage_row():
        for d in range(1, NX):
            x_out(d).wait_recv()
        one = (qpow[x, 0], qpow[x, 1])
        total = (xin[0, 0], xin[0, 1])
        for i in range(1, NX):
            moved = cmul(*total, *one)
            total = (moved[0] + xin[i, 0], moved[1] + xin[i, 1])
        rsum[0] = total[0]
        rsum[1] = total[1]
        for i in range(len(near_z)):
            z_out(i).start()

    def stage_near_z():
        total = (rsum[0], rsum[1])
        step = quarter_power(NX)
        power = None
        for i, d in enumerate(near_z):
            z_out(i).wait_recv()
            power = step if power is None else cmul(*power, *step)
            moved = cmul(*power, zin[i, 0], zin[i, 1])
            ok = z >= d
            total = (
                total[0] + jnp.where(ok, moved[0], 0.0),
                total[1] + jnp.where(ok, moved[1], 0.0),
            )
        wsum[0] = total[0]
        wsum[1] = total[1]
        for i in range(len(far_z)):
            z_out2(i).start()

    def stage_far_z():
        step = quarter_power(NX * radix)
        total, power = None, None
        for i, d in enumerate(far_z):
            z_out2(i).wait_recv()
            moved = (zin2[i, 0], zin2[i, 1])
            if i:
                power = step if power is None else cmul(*power, *step)
                moved = cmul(*power, *moved)
            ok = z >= d
            moved = (jnp.where(ok, moved[0], 0.0), jnp.where(ok, moved[1], 0.0))
            total = moved if total is None else (total[0] + moved[0], total[1] + moved[1])
        one = (qpow[x, 0], qpow[x, 1])
        for i in range(NX):
            sx[i, 0] = total[0]
            sx[i, 1] = total[1]
            moved = cmul(*total, *one)
            total = (moved[0] + xin[i, 0], moved[1] + xin[i, 1])
        for d in (1, 3, 2):
            x_back(d).start()
        sin[x] = sx[x]

    def stage_begin():
        for d in range(1, NX):
            x_back(d).wait_recv()
        for q in range(NX):
            beg_re[:, q * lanes : (q + 1) * lanes] = sin[q, 0]
            beg_im[:, q * lanes : (q + 1) * lanes] = sin[q, 1]

    def far_part(b, _):
        at = pl.multiple_of(b * L, L)
        total = near[pl.ds(at, L), :]
        for n in range(16):
            total += out_re[n] * beg_re[n : n + 1, :] - out_im[n] * beg_im[n : n + 1, :]
        gall[ch, pl.ds(at, L), :] = (gate[pl.ds(at, L), :].astype(jnp.float32) * total).astype(
            jnp.bfloat16
        )
        m_re, m_im = cmul(pow_re[L], pow_im[L], beg_re[...], beg_im[...])
        beg_re[...] = m_re + ent_re[b]
        beg_im[...] = m_im + ent_im[b]
        return 0

    chunk = tok // 2

    def y_copy(c, i):
        def block(dy, dev, lo=0, hi=chunk, mine=True):
            owner = lax.rem(y + dy + ny, ny) * 2 + core
            part = gall.at[owner, c * chunk + lo : c * chunk + hi]
            return remote(part, part, y_s.at[c, i], y_r.at[c, i], dev)

        mid = chunk // 2
        if i == 0:
            return block(0, other)
        if i == 1:
            return block(0, at_y(1))
        if i == 2:
            return block(0, at_y(-1))
        if i == 3:
            return block(-1, at_y(1), 0, mid)
        if i == 4:
            return block(1, at_y(-1), mid, chunk)
        if i == 5:
            return block(-1, other)
        if i == 6:
            return block(1, other)
        if i == 7:
            return block(2, other, 0, mid)
        return block(2, other, mid, chunk)

    def y_start(c):
        if ny > 1:
            for i in (1, 2, 0):
                y_copy(c, i).start()

    def y_forward(c):
        if ny > 1:
            for i in (1, 2):
                y_copy(c, i).wait_recv()
                y_copy(c, 2 + i).start()
                y_copy(c, 4 + i).start()

    def y_last(c):
        if ny > 1:
            for i in (3, 4):
                y_copy(c, i).wait_recv()
                y_copy(c, 4 + i).start()

    mid_block = blocks // 2

    def far_chunk(c):
        lax.fori_loop(c * mid_block, (c + 1) * mid_block, far_part, 0)
        y_start(c)

    def stage_1():
        stage_row()
        filters()

    def stage_2():
        stage_near_z()
        lax.fori_loop(0, mid_block, near_part, 0)

    def stage_3():
        stage_far_z()
        lax.fori_loop(mid_block, blocks, near_part, 0)

    def stage_4():
        stage_begin()
        far_chunk(0)

    def stage_5():
        far_chunk(1)

    def stage_6():
        y_forward(0)

    def stage_7():
        y_forward(1)
        y_last(0)

    def stage_8():
        y_last(1)

    stages = (stage_1, stage_2, stage_3, stage_4, stage_5, stage_6, stage_7, stage_8)

    def w_step(k):
        for dirn, (sgn, lim) in enumerate(zlim):

            @pl.when(k <= lim)
            def _():
                src_z = origin(sgn, k)
                idx = dirn * zlim[0][1] + k
                bz_step(dirn, k, sgn, src_z).wait_recv()

                @pl.when(k < lim)
                def _():
                    bz_step(dirn, k + 1, sgn, src_z).start()

                for side in range(2):
                    bx_step(idx, src_z, side, x).start()
                for sub in range(2):
                    a_step(dirn, k, sub, sgn, src_z).wait_recv()

                    @pl.when(k < lim)
                    def _():
                        a_step(dirn, k + 1, sub, sgn, src_z).start()

        before = k - 1
        halves(before, origin(1, before))

        @pl.when(jnp.logical_and(before >= 1, before <= zlim[1][1]))
        def _():
            halves(zlim[0][1] + before, origin(-1, before))

    steps = zlim[0][1]

    def tick(k, _):
        for i, stage in enumerate(stages):
            pl.when(k == i + 1)(stage)
        pl.when(k <= steps)(lambda: w_step(k))
        return 0

    lax.fori_loop(1, max(steps, len(stages)) + 1, tick, 0)
    halves(steps, origin(1, steps))

    for d in range(1, NX):
        a_first(d).wait_send()
        x_out(d).wait_send()
        x_back(d).wait_send()
    for i in range(len(near_z)):
        z_out(i).wait_send()
    for i in range(len(far_z)):
        z_out2(i).wait_send()

    def finish(k, _):
        for dirn, (sgn, lim) in enumerate(zlim):

            @pl.when(k <= lim)
            def _():
                src_z = origin(sgn, k - 1)
                bz_step(dirn, k, sgn, src_z).wait_send()
                for sub in range(2):
                    a_step(dirn, k, sub, sgn, src_z).wait_send()

        return 0

    lax.fori_loop(1, steps + 1, finish, 0)

    def finish_x(idx, _):
        off = jnp.where(idx <= steps, idx, steps - idx)
        src_z = lax.rem(z - off + nz, nz)
        for side in range(2):
            here = x - 1 if side == 0 else x + 1
            bx_step(idx, src_z, side, x).wait_send()
            bh_step(idx, src_z, side, here).wait_send()
            bh_step(idx, src_z, side, x + 2).wait_recv()
        return 0

    lax.fori_loop(0, nz, finish_x, 0)
    if ny > 1:
        for c in range(2):
            for i in (0, 5, 6, 7, 8):
                y_copy(c, i).wait_recv()
            for i in range(9):
                y_copy(c, i).wait_send()

    acc[...] = jnp.zeros_like(acc)
    per = chans // rows

    def project(j, _):
        w = wfull[pl.ds(j * per, per)].reshape(chans, chans)
        acc[...] += jnp.dot(gall[j], w, preferred_element_type=jnp.float32)
        return 0

    lax.fori_loop(0, gall.shape[0], project, 0)
    out[...] = acc[...].astype(out.dtype)


def on_device(
    gate_input, key_input, value_input, decay_rate, frequency, residue, skip_gain, out_weight
):
    n_ctx, n_ch = lax.axis_size("ctx"), lax.axis_size("ch")
    nz, ny = n_ctx // NX, n_ch // 2
    radix = {16: 4, 4: 2}[nz]
    tok, chans = key_input.shape
    rows = out_weight.shape[0]
    modes = decay_rate.shape[0]
    lanes = chans // NX
    f32, bf16 = jnp.float32, jnp.bfloat16
    dma = pltpu.SemaphoreType.DMA
    steps = nz // 2
    state = (2, modes, lanes)
    vmem = pl.BlockSpec(memory_space=pltpu.VMEM)
    scratch = [
        pltpu.VMEM((n_ctx, rows, chans), bf16),
        pltpu.VMEM((n_ch, tok, chans), bf16),
        pltpu.VMEM((tok, chans), f32),
        pltpu.VMEM((tok, chans), f32),
        pltpu.VMEM((tok, chans), f32),
        pltpu.VMEM((L + 1, modes, chans), f32),
        pltpu.VMEM((L + 1, modes, chans), f32),
        pltpu.VMEM((modes, L, chans), f32),
        pltpu.VMEM((modes, L, chans), f32),
        pltpu.VMEM((L, L, chans), f32),
        pltpu.VMEM((2 * L, chans), f32),
        pltpu.VMEM((tok // L, modes, chans), f32),
        pltpu.VMEM((tok // L, modes, chans), f32),
        pltpu.VMEM((modes, chans), f32),
        pltpu.VMEM((modes, chans), f32),
        pltpu.VMEM((modes, chans), f32),
        pltpu.VMEM((modes, chans), f32),
        pltpu.VMEM((NX,) + state, f32),
        pltpu.VMEM((2, modes, chans), f32),
        pltpu.VMEM((NX,) + state, f32),
        pltpu.VMEM((NX,) + state, f32),
        pltpu.VMEM((radix - 1,) + state, f32),
        pltpu.VMEM((radix,) + state, f32),
        pltpu.VMEM(state, f32),
        pltpu.VMEM(state, f32),
        pltpu.VMEM((NX,) + state, f32),
        pltpu.VMEM((NX,) + state, f32),
        dma((3,)),
        dma((3,)),
        dma((2, steps + 1, 2)),
        dma((2, steps + 1, 2)),
        dma((2, steps + 1)),
        dma((2, steps + 1)),
        dma((nz, 2)),
        dma((nz, 2)),
        dma((nz, 2)),
        dma((nz, 2)),
        dma((13,)),
        dma((13,)),
        dma((2, 9)),
        dma((2, 9)),
    ]
    return pl.pallas_call(
        functools.partial(kernel, (nz, ny, radix)),
        out_shape=jax.ShapeDtypeStruct((tok, chans), bf16),
        in_specs=[vmem] * 8,
        out_specs=vmem,
        scratch_shapes=scratch,
        compiler_params=pltpu.CompilerParams(
            collective_id=0, has_side_effects=True, vmem_limit_bytes=40 << 20
        ),
    )(
        gate_input,
        key_input,
        value_input,
        decay_rate,
        frequency,
        residue,
        skip_gain.reshape(1, chans),
        out_weight,
    )


def solution(mesh):
    placed = (
        P("ctx", "ch"),
        P("ctx", "ch"),
        P("ctx", "ch"),
        P(None, "ch"),
        P(None, "ch"),
        P(None, None, "ch"),
        P("ch"),
        P("ctx", "ch"),
    )
    return jax.shard_map(
        on_device, mesh=mesh, in_specs=placed, out_specs=P("ctx", "ch"), check_vma=False
    )
```

time: 918 us -> 75.8 us (0.08)
  the two profiles are of different devices: /device:TPU:16 before, /device:TPU:2 now
where the time goes in v1:
time: 75.8 us; the launch traced here: 75.3 us
  Pallas kernels  67.9 us (90%)
  local copies, waits for them, and re-layouts  7.43 us (10%)
    pallas_call x1, Pallas kernels, on_device(): pl.pallas_call(functools.partial(kernel, (nz, ny, radix)), out_shape=jax....  67.9 us
    unnamed x17, local copies, waits for them, and re-layouts  7.43 us

profile of v1, /device:TPU:2, one launch (start us, length us, event | category | flops | bytes accessed | tf_op | source)
XLA Modules:
  0.0 75.3 jit_solution(8039155723152927995)
XLA Ops:
  0.0 0.0 copy-start
  0.0 0.9 %copy-done = bf16[256,512]{1,0:T(8,128)(2,1)S(1)} copy-done((bf16[256,512]{1,0:T(8,128)(2,1)S(1)}, bf16[256,512]{1,0:T(8,128)(2,1)}, u32[]{:S(2)}) %copy-start) | copy-done | bytes 262168
  1.0 0.0 copy-start.1
  1.0 0.9 %copy-done.1 = bf16[256,512]{1,0:T(8,128)(2,1)S(1)} copy-done((bf16[256,512]{1,0:T(8,128)(2,1)S(1)}, bf16[256,512]{1,0:T(8,128)(2,1)}, u32[]{:S(2)}) %copy-start.1) | copy-done | bytes 262168
  1.9 0.0 copy-start.2
  1.9 0.9 %copy-done.2 = bf16[256,512]{1,0:T(8,128)(2,1)S(1)} copy-done((bf16[256,512]{1,0:T(8,128)(2,1)S(1)}, bf16[256,512]{1,0:T(8,128)(2,1)}, u32[]{:S(2)}) %copy-start.2) | copy-done | bytes 262168
  2.9 0.0 copy-start.3
  2.9 0.8 %copy-done.3 = f32[2,16,512]{2,1,0:T(8,128)S(1)} copy-done((f32[2,16,512]{2,1,0:T(8,128)S(1)}, f32[2,16,512]{2,1,0:T(8,128)}, u32[]{:S(2)}) %copy-start.3) | copy-done | bytes 65560
  3.7 0.0 copy-start.4
  3.7 0.8 %copy-done.4 = bf16[64,512]{1,0:T(8,128)(2,1)S(1)} copy-done((bf16[64,512]{1,0:T(8,128)(2,1)S(1)}, bf16[64,512]{1,0:T(8,128)(2,1)}, u32[]{:S(2)}) %copy-start.4) | copy-done | bytes 65560
  4.5 0.0 copy-start.5
  4.5 0.8 %copy-done.5 = f32[16,512]{1,0:T(8,128)S(1)} copy-done((f32[16,512]{1,0:T(8,128)S(1)}, f32[16,512]{1,0:T(8,128)}, u32[]{:S(2)}) %copy-start.5) | copy-done | bytes 32792
  5.3 0.0 copy-start.6
  5.3 0.8 %copy-done.6 = f32[16,512]{1,0:T(8,128)S(1)} copy-done((f32[16,512]{1,0:T(8,128)S(1)}, f32[16,512]{1,0:T(8,128)}, u32[]{:S(2)}) %copy-start.6) | copy-done | bytes 32792
  6.0 0.0 copy-start.7
  6.1 0.7 copy-done.7
  6.7 67.9 %shard_map.82 = bf16[256,512]{1,0:T(8,128)(2,1)S(1)} custom-call(bf16[256,512]{1,0:T(8,128)(2,1)S(1)} %copy-done, bf16[256,512]{1,0:T(8,128)(2,1)S(1)} %copy-done.1, bf16[256,512]{1,0:T(8,128)(2,1)S(1)} %copy-done.2, f32[16,512]{1,0:T(8,128)S(1)} %copy-done.5, f32[16,512]{1,0:T(8,128)S(1)} %copy-done.6, f32[2,16,512]{2,1,0:T(8,128)S(1)} %copy-done.3, ...), custom_call_target="tpu_custom_call" | custom-call | tf_op jit(solution)/shard_map/pallas_call | solution.py:541
  74.6 0.7 copy.10
Async XLA Ops:
  0.0 0.9 %copy-start = (bf16[256,512]{1,0:T(8,128)(2,1)S(1)}, bf16[256,512]{1,0:T(8,128)(2,1)}, u32[]{:S(2)}) copy-start(bf16[256,512]{1,0:T(8,128)(2,1)} %gate.1) | copy-start | bytes 786436
  1.0 0.9 %copy-start.1 = (bf16[256,512]{1,0:T(8,128)(2,1)S(1)}, bf16[256,512]{1,0:T(8,128)(2,1)}, u32[]{:S(2)}) copy-start(bf16[256,512]{1,0:T(8,128)(2,1)} %key.1) | copy-start | bytes 786436
  1.9 0.9 %copy-start.2 = (bf16[256,512]{1,0:T(8,128)(2,1)S(1)}, bf16[256,512]{1,0:T(8,128)(2,1)}, u32[]{:S(2)}) copy-start(bf16[256,512]{1,0:T(8,128)(2,1)} %value.1) | copy-start | bytes 786436
  2.9 0.8 %copy-start.3 = (f32[2,16,512]{2,1,0:T(8,128)S(1)}, f32[2,16,512]{2,1,0:T(8,128)}, u32[]{:S(2)}) copy-start(f32[2,16,512]{2,1,0:T(8,128)} %residue.1) | copy-start | bytes 196612
  3.7 0.8 %copy-start.4 = (bf16[64,512]{1,0:T(8,128)(2,1)S(1)}, bf16[64,512]{1,0:T(8,128)(2,1)}, u32[]{:S(2)}) copy-start(bf16[64,512]{1,0:T(8,128)(2,1)} %weight.1) | copy-start | bytes 196612
  4.5 0.8 %copy-start.5 = (f32[16,512]{1,0:T(8,128)S(1)}, f32[16,512]{1,0:T(8,128)}, u32[]{:S(2)}) copy-start(f32[16,512]{1,0:T(8,128)} %decay.1) | copy-start | bytes 98308
  5.3 0.8 %copy-start.6 = (f32[16,512]{1,0:T(8,128)S(1)}, f32[16,512]{1,0:T(8,128)}, u32[]{:S(2)}) copy-start(f32[16,512]{1,0:T(8,128)} %freq.1) | copy-start | bytes 98308
  6.0 0.7 copy-start.7

commit v2 on v0

v2 whole, which is shorter than its diff:
```python
import functools

import jax
import jax.numpy as jnp
from jax import lax
from jax.experimental import pallas as pl
from jax.experimental.pallas import tpu as pltpu
from jax.sharding import PartitionSpec as P

MESH = pl.DeviceIdType.MESH
NX = 4
L = 16
NB = 8
CHUNKS = 4


def cmul(a_re, a_im, b_re, b_im):
    return (a_re * b_re - a_im * b_im, a_re * b_im + a_im * b_re)


def remote(src, dst, send_sem, recv_sem, device):
    return pltpu.make_async_remote_copy(
        src_ref=src,
        dst_ref=dst,
        send_sem=send_sem,
        recv_sem=recv_sem,
        device_id=device,
        device_id_type=MESH,
    )


def small_trig(angle):
    q = angle * angle
    cos = 1.0 + q * (-1.0 / 2 + q * (1.0 / 24 + q * (-1.0 / 720 + q * (1.0 / 40320))))
    sin = angle * (1.0 + q * (-1.0 / 6 + q * (1.0 / 120 + q * (-1.0 / 5040 + q * (1.0 / 362880)))))
    return cos, sin


def kernel(
    cfg,
    gate_h, key_h, value_h, decay_h, freq_h, residue_h, skip_h, weight_h,
    out,
    wfull, gall, gate, key, value, decay, freq, residue, skip,
    sig, near, acc,
    pow_re, pow_im, out_re, out_im, toep, hpad,
    ent_re, ent_im, beg_re, beg_im, cur_re, cur_im, co_re, co_im,
    esend, qpow, xin, zin, rsum, sx, sin,
    in_s, know, ax_s, ax_r, az_s, az_r, bz_s, bz_r, bx_s, bx_r,
    xo_s, xo_r, zo_s, zo_r, xb_s, xb_r, y_s, y_r,
):
    nz, ny = cfg
    tok, chans = key.shape
    modes = decay.shape[0]
    blocks = tok // L
    nb = min(NB, blocks)
    lanes = chans // NX
    rows = wfull.shape[1]
    ra = rows // 2
    steps = nz // 2
    zlim = ((1, steps), (-1, steps - 1))
    chunks = min(CHUNKS, blocks)
    chunk = tok // chunks
    per_chunk = blocks // chunks

    ctx = lax.axis_index("ctx")
    ch = lax.axis_index("ch")
    z, x = ctx // NX, lax.rem(ctx, NX)
    y, core = ch // 2, lax.rem(ch, 2)

    def wrap(value, size):
        value = jnp.where(value < 0, value + size, value)
        return jnp.where(value >= size, value - size, value)

    z_at = {d: (wrap(z + d, nz) * NX + x, ch) for d in range(1 - nz, nz)}
    x_of = {d: wrap(x + d, NX) for d in range(1 - NX, NX)}
    x_at = {d: (z * NX + x_of[d], ch) for d in x_of}
    y_of = {d: wrap(y + d, ny) * 2 + core for d in (-1, 0, 1, 2)}
    y_at = {d: (ctx, y_of[d]) for d in y_of}
    at_z, at_x, at_y = z_at.get, x_at.get, y_at.get
    other = (ctx, y * 2 + 1 - core)

    fetches = [
        pltpu.make_async_copy(src, dst, in_s.at[i])
        for i, (src, dst) in enumerate(
            (
                (decay_h, decay),
                (freq_h, freq),
                (key_h, key),
                (value_h, value),
                (weight_h, wfull.at[ctx]),
                (residue_h, residue),
                (skip_h, skip),
                (gate_h, gate),
            )
        )
    ]
    for fetch in fetches:
        fetch.start()
    for d in range(nz - 1):
        zin[d] = jnp.zeros(zin.shape[1:], zin.dtype)

    peers = [at_z(1), at_z(-1)] + [at_x(d) for d in range(1, NX)]
    if ny > 1:
        peers += [at_y(1), at_y(-1), at_y(2), other]
    barrier = pltpu.get_barrier_semaphore()
    for peer in peers:
        pl.semaphore_signal(barrier, inc=1, device_id=peer, device_id_type=MESH)

    fetches[4].wait()
    pl.semaphore_wait(barrier, len(peers))

    def a_first(d):
        part = wfull.at[ctx, 0:ra]
        return remote(part, part, ax_s.at[d - 1], ax_r.at[d - 1], at_x(d))

    def bz_step(dirn, k, sgn, src_z):
        part = wfull.at[src_z * NX + x, ra:rows]
        return remote(part, part, bz_s.at[dirn, k], bz_r.at[dirn, k], at_z(sgn))

    def bx_step(idx, src_z, d, from_x):
        part = wfull.at[src_z * NX + from_x, ra:rows]
        return remote(part, part, bx_s.at[idx, d - 1], bx_r.at[idx, d - 1], at_x(d))

    def origin(sgn, k):
        return wrap(z - sgn * k, nz)

    for d in (2, 1, 3):
        a_first(d).start()
    for dirn, (sgn, lim) in enumerate(zlim):
        bz_step(dirn, 1, sgn, z).start()
    for d in (2, 1, 3):
        bx_step(0, z, d, x).start()

    def w_event(j):
        for dirn, (sgn, lim) in enumerate(zlim):

            @pl.when(j <= lim)
            def _():
                src_z = origin(sgn, j)
                bz_step(dirn, j, sgn, src_z).wait_recv()

                @pl.when(j < lim)
                def _():
                    bz_step(dirn, j + 1, sgn, src_z).start()

        @pl.when(j == 1)
        def _():
            for dirn, (sgn, lim) in enumerate(zlim):
                a_next(dirn, 1, 0, sgn, z).start()
            for d in range(1, NX):
                a_first(d).wait_recv()
                for dirn, (sgn, lim) in enumerate(zlim):
                    a_next(dirn, 1, d, sgn, z).start()

        k = j - 1
        for i in range(NX):
            for dirn, (sgn, lim) in enumerate(zlim):

                @pl.when(jnp.logical_and(k >= 1, k <= lim))
                def _():
                    src_z = origin(sgn, k)
                    a_next(dirn, k, i, sgn, src_z).wait_recv()

                    @pl.when(k < lim)
                    def _():
                        a_next(dirn, k + 1, i, sgn, src_z).start()

        for dirn, (sgn, lim) in enumerate(zlim):

            @pl.when(j <= lim)
            def _():
                for d in (2, 1, 3):
                    bx_step(dirn * steps + j, origin(sgn, j), d, x).start()

    def a_next(dirn, k, i, sgn, src_z):
        part = wfull.at[src_z * NX + x_of[-i], 0:ra]
        return remote(part, part, az_s.at[dirn, k, i], az_r.at[dirn, k, i], at_z(sgn))

    def tell(r):
        for d in (1 << r, -(1 << r)):
            pl.semaphore_signal(know.at[r], inc=1, device_id=at_z(d), device_id_type=MESH)

    rounds = steps.bit_length() - 1

    def hear(r):
        if r < rounds:
            pl.semaphore_wait(know.at[r], 2)
            if r + 1 < rounds:
                tell(r + 1)

    tell(0)

    fetches[0].wait()
    fetches[1].wait()
    damp = 0.125 * decay[...]
    turn = 0.125 * freq[...]
    fade = jnp.exp(-damp)
    cos, sine = small_trig(turn)
    lam_re, lam_im = fade * cos, fade * sine
    power = (jnp.ones_like(lam_re), jnp.zeros_like(lam_im))
    for k in range(L + 1):
        pow_re[k] = power[0]
        pow_im[k] = power[1]
        power = cmul(power[0], power[1], lam_re, lam_im)

    fetches[2].wait()
    fetches[3].wait()

    def signals(i, _):
        at = pl.multiple_of(i * L, L)
        both = key[pl.ds(at, L), :].astype(jnp.float32) * value[pl.ds(at, L), :].astype(jnp.float32)
        for g in range(NX):
            sig[g, pl.ds(at, L), :] = both[:, g * lanes : (g + 1) * lanes]
        return 0

    lax.fori_loop(0, blocks, signals, 0, unroll=2)

    def lane_group(g):
        return pl.ds(pl.multiple_of(g * lanes, lanes), lanes)

    groups = blocks // nb

    def entries(i, _):
        g = i // groups
        at, first = lane_group(g), pl.multiple_of(lax.rem(i, groups) * nb * L, nb * L)
        totals = [[jnp.zeros((modes, lanes), jnp.float32)] * 2 for _ in range(nb)]
        for s in range(L):
            p_re, p_im = pow_re[L - 1 - s, :, at], pow_im[L - 1 - s, :, at]
            for b in range(nb):
                row = sig[g, pl.ds(first + (b * L + s), 1), :]
                totals[b] = [totals[b][0] + p_re * row, totals[b][1] + p_im * row]
        for b in range(nb):
            ent_re[lax.rem(i, groups) * nb + b, :, at] = totals[b][0]
            ent_im[lax.rem(i, groups) * nb + b, :, at] = totals[b][1]
        return 0

    lax.fori_loop(0, NX * groups // 2, entries, 0)
    hear(0)
    lax.fori_loop(NX * groups // 2, NX * groups, entries, 0)

    def advance(b, state):
        moved = cmul(*state, pow_re[L], pow_im[L])
        return (moved[0] + ent_re[b], moved[1] + ent_im[b])

    empty = jnp.zeros((modes, chans), jnp.float32)
    whole = lax.fori_loop(0, blocks, advance, (empty, empty))
    for q in range(NX):
        for part in range(2):
            esend[q, part] = whole[part][:, q * lanes : (q + 1) * lanes]

    def x_out(d):
        to = x_of[d]
        return remote(esend.at[to], xin.at[x], xo_s.at[d - 1], xo_r.at[d - 1], at_x(d))

    def z_out(d):
        return remote(rsum, zin.at[d - 1], zo_s.at[d - 1], zo_r.at[d - 1], at_z(d))

    def x_back(d):
        to = x_of[d]
        return remote(sx.at[to], sin.at[x], xb_s.at[d - 1], xb_r.at[d - 1], at_x(d))

    for d in (2, 1, 3):
        x_out(d).start()
    xin[x] = esend[x]
    w_event(1)
    hear(1)

    fade_q = jnp.exp(-damp * float(tok))
    q_re = fade_q * jnp.cos(turn * float(tok))
    q_im = fade_q * jnp.sin(turn * float(tok))
    for q in range(NX):
        qpow[q, 0] = q_re[:, q * lanes : (q + 1) * lanes]
        qpow[q, 1] = q_im[:, q * lanes : (q + 1) * lanes]
    for i in (5, 6, 7):
        fetches[i].wait()
    scale = jnp.sqrt(2.0 * damp)
    co_re[...] = scale * residue[0]
    co_im[...] = scale * residue[1]

    place = lax.broadcasted_iota(jnp.int32, (8, chans), 0)

    def out_tables(n, total):
        def row(ref, k):
            return jnp.broadcast_to(ref[k, pl.ds(n, 1), :], (8, chans))

        c_re = jnp.broadcast_to(co_re[pl.ds(n, 1), :], (8, chans))
        c_im = jnp.broadcast_to(co_im[pl.ds(n, 1), :], (8, chans))
        v = cmul(c_re, c_im, row(pow_re, 1), row(pow_im, 1))
        for bit in (1, 2, 4):
            w = cmul(*v, row(pow_re, bit), row(pow_im, bit))
            on = (place & bit) != 0
            v = (jnp.where(on, w[0], v[0]), jnp.where(on, w[1], v[1]))
        hi = cmul(*v, row(pow_re, 8), row(pow_im, 8))
        t_re = jnp.concatenate([v[0], hi[0]], axis=0)
        out_re[n] = t_re
        out_im[n] = jnp.concatenate([v[1], hi[1]], axis=0)
        return total + t_re

    def filters():
        later = lax.fori_loop(0, modes, out_tables, jnp.zeros((L, chans), jnp.float32))
        hpad[0:L, :] = jnp.zeros((L, chans), jnp.float32)
        hpad[L - 1 : L, :] = jnp.sum(co_re[...], axis=0, keepdims=True) + skip[...]
        hpad[L : 2 * L, :] = later
        for s in range(L):
            toep[s] = hpad[L - 1 - s : 2 * L - 1 - s, :]

    def near_part(i, _):
        g = i // groups
        at, first = lane_group(g), pl.multiple_of(lax.rem(i, groups) * nb * L, nb * L)
        totals = [jnp.zeros((L, lanes), jnp.float32) for _ in range(nb)]
        for s in range(L):
            table = toep[s, :, at]
            for b in range(nb):
                totals[b] = totals[b] + table * sig[g, pl.ds(first + (b * L + s), 1), :]
        for b in range(nb):
            near[pl.ds(pl.multiple_of(first + b * L, L), L), at] = totals[b]
        return 0

    def stage_row():
        for d in range(1, NX):
            x_out(d).wait_recv()
        one = (qpow[x, 0], qpow[x, 1])
        total = (xin[0, 0], xin[0, 1])
        for i in range(1, NX):
            moved = cmul(*total, *one)
            total = (moved[0] + xin[i, 0], moved[1] + xin[i, 1])
        rsum[0] = total[0].astype(rsum.dtype)
        rsum[1] = total[1].astype(rsum.dtype)
        hear(2)
        for d in sorted(range(1, nz), key=lambda d: -min(d, nz - d)):
            pl.when(z + d < nz)(z_out(d).start)

    def stage_z():
        one = (qpow[x, 0], qpow[x, 1])
        two = cmul(*one, *one)
        step = cmul(*two, *two)
        for d in range(1, nz):
            pl.when(z >= d)(z_out(d).wait_recv)
        total = (jnp.zeros((modes, lanes), jnp.float32),) * 2
        for d in range(nz - 1, 0, -1):
            moved = cmul(*total, *step)
            total = (
                moved[0] + zin[d - 1, 0].astype(jnp.float32),
                moved[1] + zin[d - 1, 1].astype(jnp.float32),
            )
        for i in range(NX):
            sx[i, 0] = total[0]
            sx[i, 1] = total[1]
            moved = cmul(*total, *one)
            total = (moved[0] + xin[i, 0], moved[1] + xin[i, 1])
        for d in (2, 1, 3):
            x_back(d).start()
        sin[x] = sx[x]

    def stage_begin():
        for d in range(1, NX):
            x_back(d).wait_recv()
        for q in range(NX):
            cur_re[:, q * lanes : (q + 1) * lanes] = sin[q, 0]
            cur_im[:, q * lanes : (q + 1) * lanes] = sin[q, 1]

    def far_chunk(c):
        state = (cur_re[...], cur_im[...])
        for i in range(per_chunk):
            for g in range(NX):
                beg_re[g, i] = state[0][:, g * lanes : (g + 1) * lanes]
                beg_im[g, i] = state[1][:, g * lanes : (g + 1) * lanes]
            moved = cmul(*state, pow_re[L], pow_im[L])
            b = c * per_chunk + i
            state = (moved[0] + ent_re[b], moved[1] + ent_im[b])
        cur_re[...] = state[0]
        cur_im[...] = state[1]

        def far_part(g, _):
            at = lane_group(g)
            spots = [pl.ds(pl.multiple_of(c * chunk + i * L, L), L) for i in range(per_chunk)]
            totals = [near[spot, at] for spot in spots]
            for n in range(modes):
                t_re, t_im = out_re[n, :, at], out_im[n, :, at]
                for i in range(per_chunk):
                    totals[i] = totals[i] + (
                        t_re * beg_re[g, i, n : n + 1, :] - t_im * beg_im[g, i, n : n + 1, :]
                    )
            for spot, total in zip(spots, totals):
                gated = gate[spot, at].astype(jnp.float32) * total
                gall[ch, spot, at] = gated.astype(jnp.bfloat16)
            return 0

        lax.fori_loop(0, NX, far_part, 0)

    direct = chunks // 2

    def y_copy(c, i, straight):
        def block(dy, dev, lo=0, hi=chunk):
            at = c * chunk + lo
            part = gall.at[y_of[dy], pl.ds(pl.multiple_of(at, hi - lo), hi - lo)]
            return remote(part, part, y_s.at[c, i], y_r.at[c, i], dev)

        mid = chunk // 2
        if i == 0:
            return block(0, other)
        if i == 1:
            return block(0, at_y(1))
        if i == 2:
            return block(0, at_y(-1))
        if i == 3:
            return block(0, at_y(2)) if straight else block(-1, at_y(1), 0, mid)
        if i == 4:
            return block(1, at_y(-1), mid, chunk)
        if i == 5:
            return block(-1, other)
        if i == 6:
            return block(1, other)
        if i == 7:
            return block(2, other) if straight else block(2, other, 0, mid)
        return block(2, other, mid, chunk)

    def y_forward(c):
        if ny > 1:
            for i in (1, 2):
                y_copy(c, i, c >= direct).wait_recv()
                if c < direct:
                    y_copy(c, 2 + i, False).start()
                y_copy(c, 4 + i, c >= direct).start()

    def y_last(c):
        if ny > 1:
            if c < direct:
                for i in (3, 4):
                    y_copy(c, i, False).wait_recv()
                    y_copy(c, 4 + i, False).start()
            else:
                part = gall.at[y_of[2], c * chunk : (c + 1) * chunk]
                remote(part, part, y_s.at[c, 3], y_r.at[c, 3], at_y(2)).wait_recv()
                y_copy(c, 7, True).start()

    def far_all():
        def one(c, _):
            far_chunk(c)
            if ny > 1:
                for i in (1, 2, 0):
                    y_copy(c, i, False).start()

                @pl.when(c >= direct)
                def _():
                    y_copy(c, 3, True).start()

            return 0

        lax.fori_loop(0, chunks, one, 0)

    def stage_1():
        stage_row()
        filters()

    def stage_2():
        lax.fori_loop(0, NX * groups, near_part, 0)

    def stage_5():
        stage_begin()
        far_all()

    def stage_6():
        y_forward(0)
        y_forward(1)

    def stage_7():
        if chunks > 2:
            y_forward(2)
            y_forward(3)
        y_last(0)

    def stage_8():
        for c in range(1, chunks):
            y_last(c)

    stages = (stage_1, stage_2, stage_z, stage_5, stage_6, stage_7, stage_8)

    def tick(k, _):
        pl.when(k <= steps + 1)(lambda: w_event(k))
        for i, stage in enumerate(stages):
            pl.when(k == i + 2)(stage)
        return 0

    lax.fori_loop(2, max(steps, len(stages)) + 2, tick, 0)

    def across(idx, _):
        off = jnp.where(idx <= steps, idx, steps - idx)
        for d in range(1, NX):
            bx_step(idx, wrap(z - off, nz), d, x_of[-d]).wait_recv()
        return 0

    lax.fori_loop(0, nz, across, 0)

    per = chans // rows

    def project(dy, side, first=False):
        if ny > 1:
            j = y_of[dy] + (0 if side == 0 else 1 - 2 * core)
        else:
            j = 0
        w = wfull[pl.ds(j * per, per)].reshape(chans, chans)
        term = jnp.dot(gall[j], w, preferred_element_type=jnp.float32)
        acc[...] = term if first else acc[...] + term

    project(0, 0, True)
    if ny > 1:
        project(-1, 0)
        project(1, 0)
        for dy, side, waits in ((0, 1, (0,)), (-1, 1, (5,)), (1, 1, (6,)), (2, 0, ()), (2, 1, (7, 8))):
            for c in range(chunks):
                for i in waits:
                    if i < 8 or c < direct:
                        y_copy(c, i, c >= direct).wait_recv()
            project(dy, side)
    out[...] = acc[...].astype(out.dtype)

    for d in range(1, NX):
        a_first(d).wait_send()
        x_out(d).wait_send()
        x_back(d).wait_send()
    for d in range(1, nz):
        pl.when(z + d < nz)(z_out(d).wait_send)

    def finish(k, _):
        for dirn, (sgn, lim) in enumerate(zlim):

            @pl.when(k <= lim)
            def _():
                src_z = origin(sgn, k - 1)
                bz_step(dirn, k, sgn, src_z).wait_send()
                for i in range(NX):
                    a_next(dirn, k, i, sgn, src_z).wait_send()

        return 0

    lax.fori_loop(1, steps + 1, finish, 0)

    def finish_x(idx, _):
        off = jnp.where(idx <= steps, idx, steps - idx)
        for d in range(1, NX):
            bx_step(idx, wrap(z - off, nz), d, x).wait_send()
        return 0

    lax.fori_loop(0, nz, finish_x, 0)
    if ny > 1:
        for c in range(chunks):
            for i in range(9):
                if c < direct or i not in (4, 8):
                    y_copy(c, i, c >= direct).wait_send()


def on_device(
    gate_input, key_input, value_input, decay_rate, frequency, residue, skip_gain, out_weight
):
    n_ctx, n_ch = lax.axis_size("ctx"), lax.axis_size("ch")
    nz, ny = n_ctx // NX, n_ch // 2
    tok, chans = key_input.shape
    rows = out_weight.shape[0]
    modes = decay_rate.shape[0]
    lanes = chans // NX
    blocks = tok // L
    chunks = min(CHUNKS, blocks)
    f32, bf16 = jnp.float32, jnp.bfloat16
    dma = pltpu.SemaphoreType.DMA
    steps = nz // 2
    state = (2, modes, lanes)
    table = pltpu.VMEM((L + 1, modes, chans), f32)
    panel = pltpu.VMEM((tok, chans), f32)
    single = pltpu.VMEM((modes, chans), f32)
    scratch = [
        pltpu.VMEM((n_ctx, rows, chans), bf16),
        pltpu.VMEM((n_ch, tok, chans), bf16),
        pltpu.VMEM((tok, chans), bf16),
        pltpu.VMEM((tok, chans), bf16),
        pltpu.VMEM((tok, chans), bf16),
        single,
        single,
        pltpu.VMEM((2, modes, chans), f32),
        pltpu.VMEM((1, chans), f32),
        pltpu.VMEM((NX, tok, lanes), f32),
        panel,
        panel,
        table,
        table,
        pltpu.VMEM((modes, L, chans), f32),
        pltpu.VMEM((modes, L, chans), f32),
        pltpu.VMEM((L, L, chans), f32),
        pltpu.VMEM((2 * L, chans), f32),
        pltpu.VMEM((blocks, modes, chans), f32),
        pltpu.VMEM((blocks, modes, chans), f32),
        pltpu.VMEM((NX, blocks // chunks, modes, lanes), f32),
        pltpu.VMEM((NX, blocks // chunks, modes, lanes), f32),
        single,
        single,
        single,
        single,
        pltpu.VMEM((NX,) + state, f32),
        pltpu.VMEM((NX,) + state, f32),
        pltpu.VMEM((NX,) + state, f32),
        pltpu.VMEM((nz - 1,) + state, bf16),
        pltpu.VMEM(state, bf16),
        pltpu.VMEM((NX,) + state, f32),
        pltpu.VMEM((NX,) + state, f32),
        dma((8,)),
        pltpu.SemaphoreType.REGULAR((4,)),
        dma((3,)),
        dma((3,)),
        dma((2, steps + 1, NX)),
        dma((2, steps + 1, NX)),
        dma((2, steps + 1)),
        dma((2, steps + 1)),
        dma((nz, 3)),
        dma((nz, 3)),
        dma((3,)),
        dma((3,)),
        dma((nz - 1,)),
        dma((nz - 1,)),
        dma((3,)),
        dma((3,)),
        dma((chunks, 9)),
        dma((chunks, 9)),
    ]
    return pl.pallas_call(
        functools.partial(kernel, (nz, ny)),
        out_shape=jax.ShapeDtypeStruct((tok, chans), bf16),
        in_specs=[pl.BlockSpec(memory_space=pltpu.HBM)] * 8,
        out_specs=pl.BlockSpec(memory_space=pltpu.VMEM),
        scratch_shapes=scratch,
        compiler_params=pltpu.CompilerParams(
            collective_id=0, has_side_effects=True, vmem_limit_bytes=40 << 20
        ),
    )(
        *(
            pltpu.with_memory_space_constraint(array, pltpu.HBM)
            for array in (
                gate_input,
                key_input,
                value_input,
                decay_rate,
                frequency,
                residue,
                skip_gain.reshape(1, chans),
                out_weight,
            )
        )
    )


def solution(mesh):
    placed = (
        P("ctx", "ch"),
        P("ctx", "ch"),
        P("ctx", "ch"),
        P(None, "ch"),
        P(None, "ch"),
        P(None, None, "ch"),
        P("ch"),
        P("ctx", "ch"),
    )
    return jax.shard_map(
        on_device, mesh=mesh, in_specs=placed, out_specs=P("ctx", "ch"), check_vma=False
    )
```

time: 918 us -> 61.7 us (0.07)
  the two profiles are of different devices: /device:TPU:16 before, /device:TPU:32 now
where the time goes in v2:
time: 61.7 us; the launch traced here: 61.5 us
  Pallas kernels  60.8 us (99%)
  local copies, waits for them, and re-layouts  0.71 us (1%)
    pallas_call x1, Pallas kernels, on_device(): pl.pallas_call(functools.partial(kernel, (nz, ny)), out_shape=jax.ShapeDt...  60.8 us

profile of v2, /device:TPU:32, one launch (start us, length us, event | category | flops | bytes accessed | tf_op | source)
XLA Modules:
  0.0 61.5 jit_solution(16377660801932172360)
XLA Ops:
  0.0 60.8 %shard_map.82 = bf16[256,512]{1,0:T(8,128)(2,1)S(1)} custom-call(bf16[256,512]{1,0:T(8,128)(2,1)} %gate_h.1, bf16[256,512]{1,0:T(8,128)(2,1)} %key_h.1, bf16[256,512]{1,0:T(8,128)(2,1)} %value_h.1, f32[16,512]{1,0:T(8,128)} %decay_h.1, f32[16,512]{1,0:T(8,128)} %freq_h.1, f32[2,16,512]{2,1,0:T(8,128)} %residue_h.1, f32[1,512]{1,0:T(1,128)} %bitcast.1, ...), custom_call_target="tpu_custom_call" | custom-call | tf_op jit(solution)/shard_map/pallas_call | solution.py:624
  60.8 0.7 %copy.10 = bf16[256,512]{1,0:T(8,128)(2,1)} copy(bf16[256,512]{1,0:T(8,128)(2,1)S(1)} %shard_map.82) | data formatting | bytes 524288

commit v3 on v2

--- a/solution.py
+++ b/solution.py
@@ -55,7 +55,7 @@
     nb = min(NB, blocks)
     lanes = chans // NX
     rows = wfull.shape[1]
-    ra = rows // 2
+    ra = rows // 4
     steps = nz // 2
     zlim = ((1, steps), (-1, steps - 1))
     chunks = min(CHUNKS, blocks)
@@ -143,6 +143,9 @@
                 def _():
                     bz_step(dirn, j + 1, sgn, src_z).start()
 
+                for d in (2, 1, 3):
+                    bx_step(dirn * steps + j, src_z, d, x).start()
+
         @pl.when(j == 1)
         def _():
             for dirn, (sgn, lim) in enumerate(zlim):
@@ -164,13 +167,6 @@
                     @pl.when(k < lim)
                     def _():
                         a_next(dirn, k + 1, i, sgn, src_z).start()
-
-        for dirn, (sgn, lim) in enumerate(zlim):
-
-            @pl.when(j <= lim)
-            def _():
-                for d in (2, 1, 3):
-                    bx_step(dirn * steps + j, origin(sgn, j), d, x).start()
 
     def a_next(dirn, k, i, sgn, src_z):
         part = wfull.at[src_z * NX + x_of[-i], 0:ra]
@@ -236,6 +232,7 @@
 
     lax.fori_loop(0, NX * groups // 2, entries, 0)
     hear(0)
+    w_event(1)
     lax.fori_loop(NX * groups // 2, NX * groups, entries, 0)
 
     def advance(b, state):
@@ -262,7 +259,6 @@
     for d in (2, 1, 3):
         x_out(d).start()
     xin[x] = esend[x]
-    w_event(1)
     hear(1)
 
     fade_q = jnp.exp(-damp * float(tok))

time: 61.7 us -> 57.4 us (0.930)
  the two profiles are of different devices: /device:TPU:32 before, /device:TPU:2 now
where the time goes in v3:
time: 57.4 us; the launch traced here: 57.2 us
  Pallas kernels  56.5 us (98%)
  local copies, waits for them, and re-layouts  0.71 us (1%)
    pallas_call x1, Pallas kernels, on_device(): pl.pallas_call(functools.partial(kernel, (nz, ny)), out_shape=jax.ShapeDt...  56.5 us

profile of v3, /device:TPU:2, one launch (start us, length us, event | category | flops | bytes accessed | tf_op | source)
XLA Modules:
  0.0 57.2 jit_solution(10378808972722087760)
XLA Ops:
  0.0 56.5 %shard_map.82 = bf16[256,512]{1,0:T(8,128)(2,1)S(1)} custom-call(bf16[256,512]{1,0:T(8,128)(2,1)} %gate_h.1, bf16[256,512]{1,0:T(8,128)(2,1)} %key_h.1, bf16[256,512]{1,0:T(8,128)(2,1)} %value_h.1, f32[16,512]{1,0:T(8,128)} %decay_h.1, f32[16,512]{1,0:T(8,128)} %freq_h.1, f32[2,16,512]{2,1,0:T(8,128)} %residue_h.1, f32[1,512]{1,0:T(1,128)} %bitcast.1, ...), custom_call_target="tpu_custom_call" | custom-call | tf_op jit(solution)/shard_map/pallas_call | solution.py:620
  56.5 0.7 %copy.10 = bf16[256,512]{1,0:T(8,128)(2,1)} copy(bf16[256,512]{1,0:T(8,128)(2,1)S(1)} %shard_map.82) | data formatting | bytes 524288

commit v4 on v3

--- a/solution.py
+++ b/solution.py
@@ -12,6 +12,7 @@
 L = 16
 NB = 8
 CHUNKS = 4
+PIECES = 2
 
 
 def cmul(a_re, a_im, b_re, b_im):
@@ -124,10 +125,10 @@
     def origin(sgn, k):
         return wrap(z - sgn * k, nz)
 
+    for dirn, (sgn, lim) in enumerate(zlim):
+        bz_step(dirn, 1, sgn, z).start()
     for d in (2, 1, 3):
         a_first(d).start()
-    for dirn, (sgn, lim) in enumerate(zlim):
-        bz_step(dirn, 1, sgn, z).start()
     for d in (2, 1, 3):
         bx_step(0, z, d, x).start()
 
@@ -148,15 +149,14 @@
 
         @pl.when(j == 1)
         def _():
-            for dirn, (sgn, lim) in enumerate(zlim):
-                a_next(dirn, 1, 0, sgn, z).start()
             for d in range(1, NX):
                 a_first(d).wait_recv()
+            for i in range(PIECES):
                 for dirn, (sgn, lim) in enumerate(zlim):
-                    a_next(dirn, 1, d, sgn, z).start()
+                    a_next(dirn, 1, i, sgn, z).start()
 
         k = j - 1
-        for i in range(NX):
+        for i in range(PIECES):
             for dirn, (sgn, lim) in enumerate(zlim):
 
                 @pl.when(jnp.logical_and(k >= 1, k <= lim))
@@ -169,7 +169,7 @@
                         a_next(dirn, k + 1, i, sgn, src_z).start()
 
     def a_next(dirn, k, i, sgn, src_z):
-        part = wfull.at[src_z * NX + x_of[-i], 0:ra]
+        part = wfull.at[pl.ds(src_z * NX + i * (NX // PIECES), NX // PIECES), 0:ra]
         return remote(part, part, az_s.at[dirn, k, i], az_r.at[dirn, k, i], at_z(sgn))
 
     def tell(r):
@@ -525,7 +525,7 @@
             def _():
                 src_z = origin(sgn, k - 1)
                 bz_step(dirn, k, sgn, src_z).wait_send()
-                for i in range(NX):
+                for i in range(PIECES):
                     a_next(dirn, k, i, sgn, src_z).wait_send()
 
         return 0

time: 57.4 us -> 57.4 us (level)
  no operation moved by 1% of the time
where the time goes in v4:
time: 57.4 us; the launch traced here: 57.2 us
  Pallas kernels  56.5 us (98%)
  local copies, waits for them, and re-layouts  0.71 us (1%)
    pallas_call x1, Pallas kernels, on_device(): pl.pallas_call(functools.partial(kernel, (nz, ny)), out_shape=jax.ShapeDt...  56.5 us

profile of v4, /device:TPU:2, one launch (start us, length us, event | category | flops | bytes accessed | tf_op | source)
XLA Modules:
  0.0 57.2 jit_solution(16885151170732252278)
XLA Ops:
  0.0 56.5 %shard_map.82 = bf16[256,512]{1,0:T(8,128)(2,1)S(1)} custom-call(bf16[256,512]{1,0:T(8,128)(2,1)} %gate_h.1, bf16[256,512]{1,0:T(8,128)(2,1)} %key_h.1, bf16[256,512]{1,0:T(8,128)(2,1)} %value_h.1, f32[16,512]{1,0:T(8,128)} %decay_h.1, f32[16,512]{1,0:T(8,128)} %freq_h.1, f32[2,16,512]{2,1,0:T(8,128)} %residue_h.1, f32[1,512]{1,0:T(1,128)} %bitcast.1, ...), custom_call_target="tpu_custom_call" | custom-call | tf_op jit(solution)/shard_map/pallas_call | solution.py:620
  56.5 0.7 %copy.10 = bf16[256,512]{1,0:T(8,128)(2,1)} copy(bf16[256,512]{1,0:T(8,128)(2,1)S(1)} %shard_map.82) | data formatting | bytes 524288
